TPU v7x, 32 devices: a whole 2x2x4 slice. The times are simulated.
32 devices in a mesh: batch: 4 (over x, core), head: 8 (over z, y).
Axes of the slice: x: 2, y: 2, z: 4, core: 2. Of those that a mesh axis runs over, the one named last changes fastest.
Arguments:
- tokens: bfloat16 [5120, 2048], P('batch'), may hold values from -6 to 6
- segment_ids: int32 [5120], P('batch'), may hold values from 0 to 6, as said below
- norm1_gain: bfloat16 [2048], P('batch'), may hold values from 0.25 to 1.75
- w_query: bfloat16 [2048, 1024], P('batch', 'head'), may hold values from -0.125 to 0.125
- w_key: bfloat16 [2048, 512], P('batch', 'head'), may hold values from -0.125 to 0.125
- w_value: bfloat16 [2048, 512], P('batch', 'head'), may hold values from -0.125 to 0.125
- w_gate: bfloat16 [2048, 1024], P('batch', 'head'), may hold values from -0.125 to 0.125
- w_out: bfloat16 [1024, 2048], P('head', 'batch'), may hold values from -4 to 4
- norm2_gain: bfloat16 [2048], P('batch'), may hold values from 0.25 to 1.75
- w_mlp_gate: bfloat16 [2048, 6144], P('batch', 'head'), may hold values from -0.125 to 0.125
- w_mlp_up: bfloat16 [2048, 6144], P('batch', 'head'), may hold values from -0.125 to 0.125
- w_down: bfloat16 [6144, 2048], P('head', 'batch'), may hold values from -0.078125 to 0.078125
- out_grad: bfloat16 [5120, 2048], P('batch'), may hold values from -6 to 6
Outputs:
- output: bfloat16 [5120, 2048], P('batch')
- d_tokens: bfloat16 [5120, 2048], P('batch')
- d_norm1_gain: float32 [2048], P('batch')
- d_w_query: float32 [2048, 1024], P('batch', 'head')
- d_w_key: float32 [2048, 512], P('batch', 'head')
- d_w_value: float32 [2048, 512], P('batch', 'head')
- d_w_gate: float32 [2048, 1024], P('batch', 'head')
- d_w_out: float32 [1024, 2048], P('head', 'batch')
- d_norm2_gain: float32 [2048], P('batch')
- d_w_mlp_gate: float32 [2048, 6144], P('batch', 'head')
- d_w_mlp_up: float32 [2048, 6144], P('batch', 'head')
- d_w_down: float32 [6144, 2048], P('head', 'batch')
Inputs may be any that keep to these rules, and one draw needn't show every extreme that they name: `segment_ids`: segment ids never fall along the packed batch and every id from 0 to 6 occurs.
All inputs are finite; a program needn't handle non-finite values.
Results may differ from a plain program's by a relative error of at most 0.02.
Values may be sent and summed in bfloat16 or wider, within the bound.
A program may use at most 256 MiB of HBM per device.

v0:
```python
import math
import jax
import jax.numpy as jnp
from jax import lax
from jax.sharding import PartitionSpec as P

EPSILON = 1e-06
MASKED = -1e30
BF = jnp.bfloat16
F32 = jnp.float32


def from_partner(block, axis):
    count = lax.axis_size(axis)
    route = [(at, at ^ 1) for at in range(count)]
    return lax.ppermute(block, axis, route)


def matmul(left, right):
    return jnp.dot(left, right, preferred_element_type=F32)


def rows_inner(left, right):
    return lax.dot_general(left, right, (((0,), (0,)), ((), ())), preferred_element_type=F32)


def cols_inner(left, right):
    return lax.dot_general(left, right, (((1,), (1,)), ((), ())), preferred_element_type=F32)


def rms_scale(values):
    return lax.rsqrt(jnp.mean(values * values, axis=1, keepdims=True) + EPSILON)


def keep_same(state):
    return state


def order_halves(own, mate, first):
    return jnp.where(first, jnp.concatenate([own, mate], 1), jnp.concatenate([mate, own], 1))


def per_device(
    tokens,
    segment_ids,
    norm1_gain,
    w_query,
    w_key,
    w_value,
    w_gate,
    w_out,
    norm2_gain,
    w_mlp_gate,
    w_mlp_up,
    w_down,
    out_grad,
):
    heads = lax.axis_size("head")
    batches = lax.axis_size("batch")
    row_count, width = tokens.shape
    head_size = w_query.shape[1]
    half = w_key.shape[1]
    chunk = row_count // heads
    me = lax.axis_index("head")
    first = me % 2 == 0
    scale_factor = 1.0 / math.sqrt(head_size)
    kv_shard = jnp.concatenate([w_key, w_value], axis=1)
    kv_mate = from_partner(kv_shard, "head")
    w_in = jnp.concatenate(
        [
            w_query,
            order_halves(w_key, kv_mate[:, :half], first),
            order_halves(w_value, kv_mate[:, half:], first),
            w_gate,
        ],
        axis=1,
    )
    w_in = lax.all_gather(w_in, "batch", axis=0, tiled=True)
    gains = lax.all_gather(jnp.stack([norm1_gain, norm2_gain]), "batch", axis=1, tiled=True)
    gain_one = gains[0].astype(F32)
    gain_two = gains[1].astype(F32)
    out_own = lax.all_gather(w_out, "batch", axis=1, tiled=True)
    out_full = lax.all_gather(out_own, "head", axis=0, tiled=True)
    mgate_full = lax.all_gather(w_mlp_gate, "batch", axis=0, tiled=True)
    mup_full = lax.all_gather(w_mlp_up, "batch", axis=0, tiled=True)
    down_full = lax.all_gather(w_down, "batch", axis=1, tiled=True)
    positions = lax.axis_index("batch") * row_count + jnp.arange(row_count, dtype=jnp.int32)
    inputs = tokens.astype(F32)
    recip_one = rms_scale(inputs)
    normed_one = (inputs * recip_one * gain_one).astype(BF)
    projected = matmul(normed_one, w_in)
    queries = projected[:, :head_size].astype(BF)
    kv_local = projected[:, head_size : 3 * head_size].astype(BF)
    gate_vals = jax.nn.sigmoid(projected[:, 3 * head_size :])
    kv_all = lax.all_gather(kv_local, "batch", axis=0, tiled=True)
    seg_all = lax.all_gather(segment_ids, "batch", axis=0, tiled=True)
    block_rows = row_count
    block_total = batches

    def block_parts(block_index):
        first_row = block_index * block_rows
        key_block = kv_all[first_row : first_row + block_rows, :head_size]
        value_block = kv_all[first_row : first_row + block_rows, head_size:]
        seg_block = seg_all[first_row : first_row + block_rows]
        key_pos = first_row + jnp.arange(block_rows, dtype=jnp.int32)
        allowed = (segment_ids[:, None] == seg_block[None, :]) & (
            key_pos[None, :] <= positions[:, None]
        )
        scores = cols_inner(queries, key_block) * scale_factor
        return (scores, allowed, key_block, value_block)

    def is_live(block_index):
        first_row = block_index * block_rows
        return (first_row <= positions[-1]) & (
            seg_all[first_row + block_rows - 1] >= segment_ids[0]
        )

    run_max = jnp.full((row_count,), MASKED, F32)
    run_sum = jnp.zeros((row_count,), F32)
    for block_index in range(block_total):

        def grow(state, block_index=block_index):
            old_max, old_sum = state
            scores, allowed, key_block, value_block = block_parts(block_index)
            new_max = jnp.maximum(old_max, jnp.max(jnp.where(allowed, scores, MASKED), axis=1))
            weights = jnp.where(allowed, jnp.exp(scores - new_max[:, None]), 0.0)
            return (new_max, old_sum * jnp.exp(old_max - new_max) + jnp.sum(weights, axis=1))

        run_max, run_sum = lax.cond(is_live(block_index), grow, keep_same, (run_max, run_sum))
    log_total = run_max + jnp.log(run_sum)

    def probs_of(block_index):
        scores, allowed, key_block, value_block = block_parts(block_index)
        return (
            jnp.where(allowed, jnp.exp(scores - log_total[:, None]), 0.0),
            key_block,
            value_block,
        )

    attended = jnp.zeros((row_count, head_size), F32)
    for block_index in range(block_total):

        def accumulate(running, block_index=block_index):
            probs, key_block, value_block = probs_of(block_index)
            return running + matmul(probs.astype(BF), value_block)

        attended = lax.cond(is_live(block_index), accumulate, keep_same, attended)
    mixed = (attended * gate_vals).astype(BF)
    mixed_all = lax.all_gather(mixed, "head", axis=1, tiled=True)
    resid = inputs + matmul(mixed_all, out_full)
    recip_two = rms_scale(resid)
    normed_two = (resid * recip_two * gain_two).astype(BF)
    resid_own = lax.dynamic_slice_in_dim(resid, me * chunk, chunk, 0)
    recip_own = lax.dynamic_slice_in_dim(recip_two, me * chunk, chunk, 0)
    mixed_own = lax.dynamic_slice_in_dim(mixed_all, me * chunk, chunk, 0)
    dy_own = lax.dynamic_slice_in_dim(out_grad, me * chunk, chunk, 0).astype(F32)
    gate_pre = matmul(normed_two, mgate_full)
    up_pre = matmul(normed_two, mup_full)
    sig_gate = jax.nn.sigmoid(gate_pre)
    silu_gate = gate_pre * sig_gate
    hidden = (silu_gate * up_pre).astype(BF)
    d_hidden = cols_inner(out_grad, down_full)
    d_gate_pre = (d_hidden * up_pre * sig_gate * (1.0 + gate_pre * (1.0 - sig_gate))).astype(BF)
    d_up_pre = (d_hidden * silu_gate).astype(BF)
    dn2_part = cols_inner(d_gate_pre, mgate_full) + cols_inner(d_up_pre, mup_full)
    dn2 = lax.psum_scatter(dn2_part.astype(BF), "head", scatter_dimension=0, tiled=True).astype(F32)
    mlp_part = matmul(hidden, down_full).astype(BF)
    mlp_own = lax.psum_scatter(mlp_part, "head", scatter_dimension=0, tiled=True).astype(F32)
    output = lax.all_gather((resid_own + mlp_own).astype(BF), "head", axis=0, tiled=True)
    d_gain_two = jnp.sum(dn2 * resid_own * recip_own, axis=0)
    weighted_two = gain_two * dn2
    d_resid = (
        dy_own
        + recip_own * weighted_two
        - resid_own * recip_own**3 * jnp.mean(weighted_two * resid_own, axis=1, keepdims=True)
    )
    d_resid_low = d_resid.astype(BF)
    d_mixed_all = cols_inner(d_resid_low, out_full).astype(BF)
    d_mixed = lax.all_to_all(d_mixed_all, "head", split_axis=1, concat_axis=0, tiled=True).astype(
        F32
    )
    d_out_part = rows_inner(mixed_own, d_resid_low).astype(BF)
    d_out_head = lax.psum_scatter(d_out_part, "head", scatter_dimension=0, tiled=True)
    d_attended = (d_mixed * gate_vals).astype(BF)
    d_gate_logit = (d_mixed * attended * gate_vals * (1.0 - gate_vals)).astype(BF)
    delta = jnp.zeros((row_count,), F32)
    for block_index in range(block_total):

        def delta_add(running, block_index=block_index):
            probs, key_block, value_block = probs_of(block_index)
            return running + jnp.sum(probs * cols_inner(d_attended, value_block), axis=1)

        delta = lax.cond(is_live(block_index), delta_add, keep_same, delta)
    d_queries = jnp.zeros((row_count, head_size), F32)
    grad_pieces = []
    for block_index in range(block_total):

        def block_grads(running, block_index=block_index):
            probs, key_block, value_block = probs_of(block_index)
            d_probs = cols_inner(d_attended, value_block)
            d_scores = (probs * (d_probs - delta[:, None]) * scale_factor).astype(BF)
            d_key_block = rows_inner(d_scores, queries)
            d_value_block = rows_inner(probs.astype(BF), d_attended)
            return (
                running + matmul(d_scores, key_block),
                jnp.concatenate([d_key_block, d_value_block], axis=1).astype(BF),
            )

        def block_empty(running):
            return (running, jnp.zeros((block_rows, 2 * head_size), BF))

        d_queries, grad_piece = lax.cond(is_live(block_index), block_grads, block_empty, d_queries)
        grad_pieces.append(grad_piece)
    d_kv_all = jnp.concatenate(grad_pieces, axis=0)
    d_kv_own = lax.psum_scatter(d_kv_all, "batch", scatter_dimension=0, tiled=True)
    d_kv_mate = from_partner(d_kv_own, "head")
    d_kv = (d_kv_own.astype(F32) + d_kv_mate.astype(F32)).astype(BF)
    d_cat = jnp.concatenate(
        [
            d_queries.astype(BF),
            jnp.where(first, d_kv[:, :half], d_kv[:, half:head_size]),
            jnp.where(first, d_kv[:, head_size : head_size + half], d_kv[:, head_size + half :]),
            d_gate_logit,
        ],
        axis=1,
    )
    w_key_own = jnp.where(
        first, w_in[:, head_size : head_size + half], w_in[:, head_size + half : 2 * head_size]
    )
    w_value_own = jnp.where(
        first,
        w_in[:, 2 * head_size : 2 * head_size + half],
        w_in[:, 2 * head_size + half : 3 * head_size],
    )
    w_cat = jnp.concatenate(
        [w_in[:, :head_size], w_key_own, w_value_own, w_in[:, 3 * head_size :]], axis=1
    )
    dn1_part = cols_inner(d_cat, w_cat).astype(BF)
    dn1 = lax.psum_scatter(dn1_part, "head", scatter_dimension=0, tiled=True).astype(F32)
    inputs_own = lax.dynamic_slice_in_dim(inputs, me * chunk, chunk, 0)
    recip_in = lax.dynamic_slice_in_dim(recip_one, me * chunk, chunk, 0)
    d_gain_one = jnp.sum(dn1 * inputs_own * recip_in, axis=0)
    weighted_one = gain_one * dn1
    d_tokens = (
        d_resid
        + recip_in * weighted_one
        - inputs_own * recip_in**3 * jnp.mean(weighted_one * inputs_own, axis=1, keepdims=True)
    ).astype(BF)
    d_tokens = lax.all_gather(d_tokens, "head", axis=0, tiled=True)
    d_mlp = jnp.concatenate(
        [
            rows_inner(normed_two, d_gate_pre).astype(BF),
            rows_inner(normed_two, d_up_pre).astype(BF),
        ],
        1,
    )
    d_mlp = lax.psum_scatter(d_mlp, "batch", scatter_dimension=0, tiled=True).astype(F32)
    d_down = rows_inner(hidden, out_grad).astype(BF)
    d_down = lax.psum_scatter(d_down, "batch", scatter_dimension=1, tiled=True).astype(F32)
    d_in = rows_inner(normed_one, d_cat).astype(BF)
    d_in = lax.psum_scatter(d_in, "batch", scatter_dimension=0, tiled=True).astype(F32)
    d_out = lax.psum_scatter(d_out_head, "batch", scatter_dimension=1, tiled=True).astype(F32)
    d_gains = lax.psum(jnp.stack([d_gain_one, d_gain_two]), ("batch", "head"))
    d_gains = lax.dynamic_slice_in_dim(
        d_gains, lax.axis_index("batch") * norm1_gain.shape[0], norm1_gain.shape[0], 1
    )
    hidden_own = w_mlp_gate.shape[1]
    return (
        output,
        d_tokens,
        d_gains[0],
        d_in[:, :head_size],
        d_in[:, head_size : head_size + half],
        d_in[:, head_size + half : 2 * head_size],
        d_in[:, 2 * head_size :],
        d_out,
        d_gains[1],
        d_mlp[:, :hidden_own],
        d_mlp[:, hidden_own:],
        d_down,
    )


def solution(mesh):
    return jax.shard_map(
        per_device,
        mesh=mesh,
        in_specs=(
            P("batch", None),
            P("batch"),
            P("batch"),
            P("batch", "head"),
            P("batch", "head"),
            P("batch", "head"),
            P("batch", "head"),
            P("head", "batch"),
            P("batch"),
            P("batch", "head"),
            P("batch", "head"),
            P("head", "batch"),
            P("batch", None),
        ),
        out_specs=(
            P("batch", None),
            P("batch", None),
            P("batch"),
            P("batch", "head"),
            P("batch", "head"),
            P("batch", "head"),
            P("batch", "head"),
            P("head", "batch"),
            P("batch"),
            P("batch", "head"),
            P("batch", "head"),
            P("head", "batch"),
        ),
        check_vma=False,
    )
```

profile of v0, /device:TPU:0, one launch (start us, length us, event | category | flops | bytes accessed | tf_op | source)
XLA Modules:
  0.0 1231.5 jit_solution(9865374111591020541)
XLA Ops:
  9.3 3.0 collective-permute-start
  12.3 3.5 collective-permute-done
  19.5 5.2 all_gather.37
  24.7 3.9 multiply_reduce_fusion.1
  28.6 13.7 %all-gather.11.cloned.1.call-done = bf16[2048,512]{1,0:T(8,128)(2,1)} async-done(((bf16[512,512]{1,0:T(8,128)(2,1)}), bf16[2048,512]{1,0:T(8,128)(2,1)}) %all-gather.11.cloned.1.call-update) | async-done | bytes 2097168 | tf_op jit(solution)/shard_map/all_gather | solution.py:78
  42.3 7.8 fusion.167
  51.1 7.6 all_gather.41
  59.9 5.2 all-gather
  73.6 3.3 all-gather.13.cloned.1.call-done
  76.8 8.3 conditional.16
  76.8 3.0 copy.141
  82.2 2.9 select_reduce_fusion
  86.0 6.3 conditional.20
  86.0 3.1 copy.149
  89.2 3.2 fusion.10
  99.6 52.8 %all-gather.17.cloned.1.call-done = bf16[1024,2048]{1,0:T(8,128)(2,1)} async-done(((bf16[128,2048]{1,0:T(8,128)(2,1)}), bf16[1024,2048]{1,0:T(8,128)(2,1)}) %all-gather.17.cloned.1.call-update) | async-done | bytes 4194320 | tf_op jit(solution)/shard_map/all_gather | solution.py:83
  152.4 55.6 %all-gather.15.cloned.1.call-done = bf16[1280,1024]{0,1:T(8,128)(2,1)} async-done(((bf16[1280,128]{0,1:T(8,128)(2,1)}), bf16[1280,1024]{0,1:T(8,128)(2,1)}) %all-gather.15.cloned.1.call-update) | async-done | bytes 2621456 | tf_op jit(solution)/shard_map/all_gather | solution.py:149
  208.0 10.4 multiply_reduce_fusion
  218.4 3.9 copy-done.3
  222.3 3.3 multiply_convert_fusion
  225.6 10.9 all-gather.19.cloned.1.call-done
  236.5 9.6 fusion.168
  246.2 20.4 %all-gather.21.cloned.1.call-done = bf16[2048,768]{1,0:T(8,128)(2,1)} async-done(((bf16[512,768]{1,0:T(8,128)(2,1)}), bf16[2048,768]{1,0:T(8,128)(2,1)}) %all-gather.21.cloned.1.call-update) | async-done | bytes 3145744 | tf_op jit(solution)/shard_map/all_gather | solution.py:85
  266.5 9.6 fusion.169
  276.1 20.6 %all-gather.23.cloned.1.call-done = bf16[768,2048]{1,0:T(8,128)(2,1)} async-done(((bf16[768,512]{1,0:T(8,128)(2,1)}), bf16[768,2048]{1,0:T(8,128)(2,1)}) %all-gather.23.cloned.1.call-update) | async-done | bytes 3145744 | tf_op jit(solution)/shard_map/all_gather | solution.py:86
  296.6 13.6 %multiply_convert_fusion.2 = (bf16[1280,768]{1,0:T(8,128)(2,1)}, bf16[1280,768]{1,0:T(8,128)(2,1)}, bf16[1280,768]{1,0:T(8,128)(2,1)S(1)}) fusion(f32[1280,768]{1,0:T(8,128)} %fusion.168, f32[1280,768]{1,0:T(8,128)} %fusion.169, bf16[1280,2048]{1,0:T(8,128)(2,1)} %param.57, bf16[768,2048]{1,0:T(8,128)(2,1)} %all-gather.23.cloned.1.call-done), kind=kOutput, calls=%fused_computation.193 | convolution fusion | flops 4041277440 | bytes 22151168 | tf_op jit(solution)/shard_map/dot_general | solution.py:28
  310.3 6.7 fusion.170
  316.9 7.7 add_convert_fusion
  324.8 7.8 convolution_convert_fusion.5
  332.7 94.8 %reduce-scatter.12.cloned.1.call-done = bf16[160,2048]{1,0:T(8,128)(2,1)} async-done(((bf16[1280,2048]{1,0:T(8,128)(2,1)}), bf16[160,2048]{1,0:T(8,128)(2,1)}) %reduce-scatter.12.cloned.1.call-update) | async-done | bytes 655376 | tf_op jit(solution)/shard_map/reduce_scatter | solution.py:166
  429.9 103.4 %reduce-scatter.10.cloned.1.call-done = bf16[160,2048]{1,0:T(8,128)(2,1)} async-done(((bf16[1280,2048]{1,0:T(8,128)(2,1)}), bf16[160,2048]{1,0:T(8,128)(2,1)}) %reduce-scatter.10.cloned.1.call-update) | async-done | bytes 655376 | tf_op jit(solution)/shard_map/reduce_scatter | solution.py:168
  533.4 3.4 fusion.144
  540.1 4.5 all-to-all-start
  544.6 10.4 all-to-all-done
  560.6 8.2 conditional.24
  563.1 3.4 fusion.45
  568.8 18.2 %conditional.28 = (f32[1280,128]{1,0:T(8,128)}, bf16[1280,256]{0,1:T(8,128)(2,1)}) conditional(s32[]{:T(128)} %bitcast.4, () %tuple.134, (s32[1280]{0:T(1024)S(1)}, s32[5120]{0:T(1024)S(1)}, s32[1280]{0:T(1024)S(1)}, bf16[5120,256]{0,1:T(8,128)(2,1)S(1)}, bf16[1280,128]{0,1:T(8,128)(2,1)S(1)}, /*index=5*/f32[1280]{0:T(1024)S(1)}, ...), branch_computations={%region_41.42_spmd, %region_42.43_spmd} | conditional | flops 2116812800 | bytes 39685136 | solution.py:212
  576.2 3.5 fusion.72
  584.2 2.8 fusion.81
  588.4 4.7 conditional.30
  593.1 8.2 conditional.31
  601.3 3.0 pad_maximum_fusion.5
  604.4 4.4 convolution_convert_fusion.6
  608.9 74.5 %reduce-scatter.14.cloned.1.call-done = bf16[1280,256]{0,1:T(8,128)(2,1)} async-done(((bf16[5120,256]{0,1:T(8,128)(2,1)}), bf16[1280,256]{0,1:T(8,128)(2,1)}) %reduce-scatter.14.cloned.1.call-update) | async-done | bytes 655376 | tf_op jit(solution)/shard_map/reduce_scatter | solution.py:215
  684.9 2.8 slice_select_fusion.1
  691.9 12.9 %collective-permute-done.1 = bf16[1280,256]{0,1:T(8,128)(2,1)S(1)} collective-permute-done((bf16[1280,256]{0,1:T(8,128)(2,1)}, bf16[1280,256]{0,1:T(8,128)(2,1)S(1)}, u32[]{:S(2)}, u32[]{:S(2)}) %collective-permute-start.1) | collective-permute-done | bytes 655392 | tf_op jit(solution)/shard_map/ppermute | solution.py:16
  705.0 6.9 convolution_convert_fusion.4
  712.4 9.1 convolution_convert_fusion.7
  721.6 7.6 convolution_convert_fusion.8
  729.2 7.1 convolution_convert_fusion.9
  736.3 3.8 pad_maximum_fusion.4
  740.8 35.7 %reduce-scatter.20.cloned.1.call-done = bf16[128,2048]{1,0:T(8,128)(2,1)} async-done(((bf16[1024,2048]{1,0:T(8,128)(2,1)}), bf16[128,2048]{1,0:T(8,128)(2,1)}) %reduce-scatter.20.cloned.1.call-update) | async-done | bytes 524304 | tf_op jit(solution)/shard_map/reduce_scatter | solution.py:183
  776.8 7.0 convolution_convert_fusion.10
  783.9 7.9 convert_element_type.190
  791.9 91.0 %reduce-scatter.16.cloned.1.call-done = bf16[160,2048]{1,0:T(8,128)(2,1)} async-done(((bf16[1280,2048]{1,0:T(8,128)(2,1)}), bf16[160,2048]{1,0:T(8,128)(2,1)}) %reduce-scatter.16.cloned.1.call-update) | async-done | bytes 655376 | tf_op jit(solution)/shard_map/reduce_scatter | solution.py:239
  884.8 2.8 fusion.141
  887.6 35.6 %reduce-scatter.26.cloned.1.call-done = bf16[768,512]{1,0:T(8,128)(2,1)} async-done(((bf16[768,2048]{1,0:T(8,128)(2,1)}), bf16[768,512]{1,0:T(8,128)(2,1)}) %reduce-scatter.26.cloned.1.call-update) | async-done | bytes 786448 | tf_op jit(solution)/shard_map/reduce_scatter | solution.py:259
  925.6 58.5 %reduce-scatter.24.cloned.1.call-done = bf16[512,1536]{0,1:T(8,128)(2,1)} async-done(((bf16[2048,1536]{0,1:T(8,128)(2,1)}), bf16[512,1536]{0,1:T(8,128)(2,1)}) %reduce-scatter.24.cloned.1.call-update) | async-done | bytes 1572880 | tf_op jit(solution)/shard_map/reduce_scatter | solution.py:257
  989.1 83.3 %all-gather.25.cloned.1.call-done = bf16[1280,2048]{1,0:T(8,128)(2,1)} async-done(((bf16[160,2048]{1,0:T(8,128)(2,1)}), bf16[1280,2048]{1,0:T(8,128)(2,1)}) %all-gather.25.cloned.1.call-update) | async-done | bytes 5242896 | tf_op jit(solution)/shard_map/all_gather | solution.py:169
  1072.4 22.2 %reduce-scatter.22.cloned.1.call-done = bf16[128,512]{1,0:T(8,128)(2,1)} async-done(((bf16[128,2048]{1,0:T(8,128)(2,1)}), bf16[128,512]{1,0:T(8,128)(2,1)}) %reduce-scatter.22.cloned.1.call-update) | async-done | bytes 131088 | tf_op jit(solution)/shard_map/reduce_scatter | solution.py:262
  1096.2 29.7 %reduce-scatter.18.cloned.1.call-done = bf16[512,384]{1,0:T(8,128)(2,1)} async-done(((bf16[2048,384]{1,0:T(8,128)(2,1)}), bf16[512,384]{1,0:T(8,128)(2,1)}) %reduce-scatter.18.cloned.1.call-update) | async-done | bytes 393232 | tf_op jit(solution)/shard_map/reduce_scatter | solution.py:261
  1130.4 41.0 %psum.7 = f32[2,2048]{1,0:T(2,128)S(1)} all-reduce(f32[2,2048]{1,0:T(2,128)S(1)} %pad_maximum_fusion.11), channel_id=1, replica_groups=mesh['batch'=4,'head'=8] {'batch','head'}, use_global_device_ids=true, to_apply=%region_54.55 | all-reduce | flops 4096 | bytes 32768 | tf_op jit(solution)/shard_map/psum | solution.py:263
  1172.1 44.2 %all-gather.27.cloned.1.call-done = bf16[1280,2048]{1,0:T(8,128)(2,1)} async-done(((bf16[160,2048]{1,0:T(8,128)(2,1)}), bf16[1280,2048]{1,0:T(8,128)(2,1)}) %all-gather.27.cloned.1.call-update) | async-done | bytes 5242896 | tf_op jit(solution)/shard_map/all_gather | solution.py:249
  1216.3 5.8 copy.270
  (156 shorter events, 73.8 us)
Async XLA Ops:
  7.2 35.1 %all-gather.11.cloned.1.call-start = ((), (), s32[]{:S(2)}) async-start(), calls=%async_computation.10 | async-start | bytes 2621440 | tf_op jit(solution)/shard_map/all_gather | solution.py:78
  9.3 6.5 collective-permute-start
  18.1 58.8 %all-gather.13.cloned.1.call-start = ((), (), s32[]{:S(2)}) async-start(), calls=%async_computation.11 | async-start | bytes 3276800 | tf_op jit(solution)/shard_map/all_gather | solution.py:95
  28.6 21.5 %copy-start.15 = (f32[1280]{0:T(1024)}, f32[1280]{0:T(1024)S(1)}, u32[]{:S(2)}) copy-start(f32[1280]{0:T(1024)S(1)} %add_rsqrt_fusion.1) | copy-start | bytes 15364
  28.6 21.5 %copy-start.12 = (f32[1,2048]{1,0:T(1,128)}, f32[1,2048]{1,0:T(1,128)S(1)}, u32[]{:S(2)}) copy-start(f32[1,2048]{1,0:T(1,128)S(1)} %get-tuple-element.895) | copy-start | bytes 24580
  42.3 8.8 copy-start.11
  42.3 16.5 %copy-start.10 = (s32[1280]{0:T(1024)S(1)}, s32[1280]{0:T(1024)}, u32[]{:S(2)}) copy-start(s32[1280]{0:T(1024)} %param.46) | copy-start | bytes 15364
  51.0 101.4 %all-gather.17.cloned.1.call-start = ((), (), s32[]{:S(2)}) async-start(), calls=%async_computation.13 | async-start | bytes 4718592 | tf_op jit(solution)/shard_map/all_gather | solution.py:83
  58.7 149.3 %all-gather.15.cloned.1.call-start = ((), (), s32[]{:S(2)}) async-start(), calls=%async_computation.12 | async-start | bytes 2949120 | tf_op jit(solution)/shard_map/all_gather | solution.py:149
  95.4 123.0 %copy-start.4 = (f32[1280,128]{0,1:T(8,128)}, f32[1280,128]{0,1:T(8,128)S(1)}, u32[]{:S(2)}) copy-start(f32[1280,128]{0,1:T(8,128)S(1)} %get-tuple-element.854) | copy-start | bytes 1966084
  97.7 138.9 %all-gather.19.cloned.1.call-start = ((), (), s32[]{:S(2)}) async-start(), calls=%async_computation.14 | async-start | bytes 3932160 | tf_op jit(solution)/shard_map/all_gather | solution.py:84
  98.3 168.2 %all-gather.21.cloned.1.call-start = ((), (), s32[]{:S(2)}) async-start(), calls=%async_computation.15 | async-start | bytes 3932160 | tf_op jit(solution)/shard_map/all_gather | solution.py:85
  98.8 197.8 %all-gather.23.cloned.1.call-start = ((), (), s32[]{:S(2)}) async-start(), calls=%async_computation.16 | async-start | bytes 3932160 | tf_op jit(solution)/shard_map/all_gather | solution.py:86
  99.6 327.8 %reduce-scatter.12.cloned.1.call-start = ((), (), s32[]{:S(2)}) async-start(), calls=%async_computation.19 | async-start | bytes 5898240 | tf_op jit(solution)/shard_map/reduce_scatter | solution.py:166
  218.4 3.9 copy-start.3
  296.6 13.6 %copy-start.17 = (bf16[2048,768]{1,0:T(8,128)(2,1)S(1)}, bf16[2048,768]{1,0:T(8,128)(2,1)}, u32[]{:S(2)}) copy-start(bf16[2048,768]{1,0:T(8,128)(2,1)} %all-gather.19.cloned.1.call-done) | copy-start | bytes 9437188
  310.2 14.5 %copy-start.19 = (bf16[1280,768]{1,0:T(8,128)(2,1)}, bf16[1280,768]{1,0:T(8,128)(2,1)S(1)}, u32[]{:S(2)}) copy-start(bf16[1280,768]{1,0:T(8,128)(2,1)S(1)} %get-tuple-element.871) | copy-start | bytes 5898244
  310.3 6.7 copy-start.18
  324.7 208.7 %reduce-scatter.10.cloned.1.call-start = ((), (), s32[]{:S(2)}) async-start(), calls=%async_computation.17 | async-start | bytes 5898240 | tf_op jit(solution)/shard_map/reduce_scatter | solution.py:168
  533.4 4.4 copy-start.6
  536.7 1.1 copy-start.1
  539.3 21.2 %copy-start = (bf16[5120,256]{0,1:T(8,128)(2,1)S(1)}, bf16[5120,256]{0,1:T(8,128)(2,1)}, u32[]{:S(2)}) copy-start(bf16[5120,256]{0,1:T(8,128)(2,1)} %all-gather.13.cloned.1.call-done) | copy-start | bytes 7864324
  540.1 15.0 %all-to-all-start = ((bf16[160,8,128]{2,0,1:T(8,128)(2,1)}), bf16[160,8,128]{2,0,1:T(8,128)(2,1)S(1)}, u32[]{:S(2)}, u32[]{:S(2)}) async-start(bf16[160,8,128]{2,0,1:T(8,128)(2,1)} %bitcast.84), calls=%async_computation.2 | async-start | bytes 655360 | tf_op jit(solution)/shard_map/all_to_all | solution.py:179
  544.6 138.8 %reduce-scatter.14.cloned.1.call-start = ((), (), s32[]{:S(2)}) async-start(), calls=%async_computation.20 | async-start | bytes 3276800 | tf_op jit(solution)/shard_map/reduce_scatter | solution.py:215
  601.3 3.1 copy-start.2
  604.4 172.1 %reduce-scatter.20.cloned.1.call-start = ((), (), s32[]{:S(2)}) async-start(), calls=%async_computation.24 | async-start | bytes 4718592 | tf_op jit(solution)/shard_map/reduce_scatter | solution.py:183
  608.9 96.1 %copy-start.8 = (bf16[1280,128]{0,1:T(8,128)(2,1)S(1)}, bf16[1280,128]{0,1:T(8,128)(2,1)}, u32[]{:S(2)}) copy-start(bf16[1280,128]{0,1:T(8,128)(2,1)} %get-tuple-element.873) | copy-start | bytes 983044
  608.9 273.9 %reduce-scatter.16.cloned.1.call-start = ((), (), s32[]{:S(2)}) async-start(), calls=%async_computation.21 | async-start | bytes 5898240 | tf_op jit(solution)/shard_map/reduce_scatter | solution.py:239
  683.4 21.4 %copy-start.7 = (bf16[1280,256]{0,1:T(8,128)(2,1)S(1)}, bf16[1280,256]{0,1:T(8,128)(2,1)}, u32[]{:S(2)}) copy-start(bf16[1280,256]{0,1:T(8,128)(2,1)} %reduce-scatter.14.cloned.1.call-done) | copy-start | bytes 1966084
  683.4 21.4 %collective-permute-start.1 = (bf16[1280,256]{0,1:T(8,128)(2,1)}, bf16[1280,256]{0,1:T(8,128)(2,1)S(1)}, u32[]{:S(2)}, u32[]{:S(2)}) collective-permute-start(bf16[1280,256]{0,1:T(8,128)(2,1)} %reduce-scatter.14.cloned.1.call-done), channel_id=1, source_target_pairs={{0,1},{1,0},{2,3},{3,2},{4,5},{5,4},{6,7},{7,6},{8,9},{9,8},{10,11... | collective-permute-start | bytes 1966088 | tf_op jit(solution)/shard_map/ppermute | solution.py:16
  711.9 211.2 %reduce-scatter.26.cloned.1.call-start = ((), (), s32[]{:S(2)}) async-start(), calls=%async_computation.27 | async-start | bytes 3932160 | tf_op jit(solution)/shard_map/reduce_scatter | solution.py:259
  721.5 262.5 %reduce-scatter.24.cloned.1.call-start = ((), (), s32[]{:S(2)}) async-start(), calls=%async_computation.26 | async-start | bytes 7864320 | tf_op jit(solution)/shard_map/reduce_scatter | solution.py:257
  721.6 7.6 copy-start.20
  740.2 36.6 %copy-start.9 = (bf16[1280,128]{0,1:T(8,128)(2,1)S(1)}, bf16[1280,128]{0,1:T(8,128)(2,1)}, u32[]{:S(2)}) copy-start(bf16[1280,128]{0,1:T(8,128)(2,1)} %copy.184) | copy-start | bytes 983044
  740.2 36.6 %copy-start.13 = (f32[1,2048]{1,0:T(1,128)S(1)}, f32[1,2048]{1,0:T(1,128)}, u32[]{:S(2)}) copy-start(f32[1,2048]{1,0:T(1,128)} %copy-done.12) | copy-start | bytes 24580
  740.2 36.6 %copy-start.16 = (f32[1280]{0:T(1024)S(1)}, f32[1280]{0:T(1024)}, u32[]{:S(2)}) copy-start(f32[1280]{0:T(1024)} %copy-done.15) | copy-start | bytes 15364
  740.2 332.2 %all-gather.25.cloned.1.call-start = ((), (), s32[]{:S(2)}) async-start(), calls=%async_computation.18 | async-start | bytes 5898240 | tf_op jit(solution)/shard_map/all_gather | solution.py:169
  740.8 353.8 %reduce-scatter.22.cloned.1.call-start = ((), (), s32[]{:S(2)}) async-start(), calls=%async_computation.25 | async-start | bytes 655360 | tf_op jit(solution)/shard_map/reduce_scatter | solution.py:262
  776.5 349.4 %reduce-scatter.18.cloned.1.call-start = ((), (), s32[]{:S(2)}) async-start(), calls=%async_computation.23 | async-start | bytes 1966080 | tf_op jit(solution)/shard_map/reduce_scatter | solution.py:261
  783.8 432.5 %all-gather.27.cloned.1.call-start = ((), (), s32[]{:S(2)}) async-start(), calls=%async_computation.22 | async-start | bytes 5898240 | tf_op jit(solution)/shard_map/all_gather | solution.py:249
  987.5 142.9 %copy-start.14 = (f32[2048]{0:T(1024)S(1)}, f32[2048]{0:T(1024)}, u32[]{:S(2)}) copy-start(f32[2048]{0:T(1024)} %get-tuple-element.857) | copy-start | bytes 24580
  1216.3 5.9 copy-start.5
Sparse Core Ops, SparseCore 0:
  18.2 24.0 all-gather.10
  51.1 25.6 all-gather.12
  79.0 73.4 all-gather.16
  155.0 52.9 all-gather.14
  209.4 27.0 all-gather.18
  237.9 28.5 all-gather.20
  268.1 28.5 all-gather.22
  324.8 102.5 reduce-scatter.11
  431.0 102.3 reduce-scatter.9
  604.5 78.8 reduce-scatter.13
  687.5 89.0 reduce-scatter.19
  780.5 102.2 reduce-scatter.15
  885.3 37.7 reduce-scatter.25
  925.7 58.3 reduce-scatter.23
  986.1 86.2 all-gather.24
  1074.8 19.7 reduce-scatter.21
  1097.7 28.1 reduce-scatter.17
  1128.6 87.6 all-gather.26
where the time goes:
time: 1240 us; the launch traced here: 1230 us
  waiting for transfers between devices  879 us (71%)
  matrix products  137 us (11%)
  blocking collectives  59.1 us (5%)
  other arithmetic  52.6 us (4%)
  local copies, waits for them, and re-layouts  51.9 us (4%)
  between operations  22.7 us (2%)
  loops' own time  18.7 us (2%)
    reduce_scatter x1, waiting for transfers between devices, per_device(): lax.psum_scatter(mlp_part, 'head', scatter_dimension=0, tiled=True)  103 us
    reduce_scatter x1, waiting for transfers between devices, per_device(): lax.psum_scatter(dn2_part.astype(BF), 'head', scatter_dimension=0, tiled=...  94.8 us
    reduce_scatter x1, waiting for transfers between devices, per_device(): lax.psum_scatter(dn1_part, 'head', scatter_dimension=0, tiled=True)  91 us
    all_gather x1, waiting for transfers between devices, per_device(): lax.all_gather((resid_own + mlp_own).astype(BF), 'head', axis=0, tiled=True)  83.3 us
    reduce_scatter x1, waiting for transfers between devices, per_device(): lax.psum_scatter(d_kv_all, 'batch', scatter_dimension=0, tiled=True)  74.5 us
    reduce_scatter x1, waiting for transfers between devices, per_device(): lax.psum_scatter(d_mlp, 'batch', scatter_dimension=0, tiled=True)  58.5 us
    all_gather x1, waiting for transfers between devices, per_device(): mixed_all = lax.all_gather(mixed, 'head', axis=1, tiled=True)  55.6 us
    all_gather x1, waiting for transfers between devices, per_device(): out_full = lax.all_gather(out_own, 'head', axis=0, tiled=True)  52.8 us
  transfers between devices with their start and end apart: 21, of which 21 were waited for; matrix products, arithmetic and copies ran while one was open for 12% of the time, Pallas kernels for 0%

commit v1 on v0

--- a/solution.py
+++ b/solution.py
@@ -8,6 +8,23 @@
 MASKED = -1e30
 BF = jnp.bfloat16
 F32 = jnp.float32
+
+
+def meet_target_up(x_in):
+    z, low, out_arr = (lax.axis_size("head"), lax.axis_index("head"), x_in.shape[0])
+    sheets = tuple(((b, (b + 1) % z) for b in range(z)))
+    items = tuple(((b, (b - 1) % z) for b in range(z)))
+    later = jnp.zeros((*x_in.shape[:0], z * out_arr, *x_in.shape[1:]), x_in.dtype)
+    later = lax.dynamic_update_slice_in_dim(later, x_in, low * out_arr, axis=0)
+    tile_out = row_out = x_in
+    a_now = z // 2
+    for q in range(1, a_now + 1):
+        tile_out = lax.ppermute(tile_out, "head", sheets)
+        later = lax.dynamic_update_slice_in_dim(later, tile_out, (low - q) % z * out_arr, axis=0)
+        if q < z - a_now:
+            row_out = lax.ppermute(row_out, "head", items)
+            later = lax.dynamic_update_slice_in_dim(later, row_out, (low + q) % z * out_arr, axis=0)
+    return later
 
 
 def from_partner(block, axis):
@@ -166,7 +183,7 @@
     dn2 = lax.psum_scatter(dn2_part.astype(BF), "head", scatter_dimension=0, tiled=True).astype(F32)
     mlp_part = matmul(hidden, down_full).astype(BF)
     mlp_own = lax.psum_scatter(mlp_part, "head", scatter_dimension=0, tiled=True).astype(F32)
-    output = lax.all_gather((resid_own + mlp_own).astype(BF), "head", axis=0, tiled=True)
+    output = meet_target_up((resid_own + mlp_own).astype(BF))
     d_gain_two = jnp.sum(dn2 * resid_own * recip_own, axis=0)
     weighted_two = gain_two * dn2
     d_resid = (

time: 1240 us -> 1150 us (0.927)
  waiting for transfers between devices: 879 us -> 772 us
  starting transfers between devices: 10.3 us -> 27.3 us
    all_gather x1 -> x0, waiting for transfers between devices: 83.3 us -> none  [per_device(): lax.all_gather((resid_own + mlp_own).astype(BF), 'head', axis=0, tiled=True)]
    ppermute x0 -> x7, waiting for transfers between devices: none -> 71.5 us  [the longest x4 71.5 us: meet_target_up(): tile_out = lax.ppermute(tile_out, 'head', sheets)]
    reduce_scatter x1, waiting for transfers between devices: 58.5 us -> 2.55 us  [per_device(): lax.psum_scatter(d_mlp, 'batch', scatter_dimension=0, tiled=True)]
    reduce_scatter x1, waiting for transfers between devices: 35.6 us -> 0.78 us  [per_device(): lax.psum_scatter(d_down, 'batch', scatter_dimension=1, tiled=True)]
    ppermute x0 -> x7, starting transfers between devices: none -> 16.8 us  [the longest x4 9.04 us: meet_target_up(): tile_out = lax.ppermute(tile_out, 'head', sheets)]
  transfers between devices with their start and end apart: 21 -> 27, of which waited for: 21 -> 24; matrix products, arithmetic and copies ran while one was open for 12% -> 14% of each run, Pallas kernels for 0% -> 0%
where the time goes in v1:
time: 1150 us; the launch traced here: 1140 us
  waiting for transfers between devices  772 us (67%)
  matrix products  136 us (12%)
  local copies, waits for them, and re-layouts  60.9 us (5%)
  blocking collectives  59 us (5%)
  other arithmetic  53.6 us (5%)
  starting transfers between devices  27.3 us (2%)
  between operations  22.4 us (2%)
    reduce_scatter x1, waiting for transfers between devices, per_device(): lax.psum_scatter(dn2_part.astype(BF), 'head', scatter_dimension=0, tiled=...  103 us
    reduce_scatter x1, waiting for transfers between devices, per_device(): lax.psum_scatter(mlp_part, 'head', scatter_dimension=0, tiled=True)  102 us
    reduce_scatter x1, waiting for transfers between devices, per_device(): lax.psum_scatter(dn1_part, 'head', scatter_dimension=0, tiled=True)  90.7 us
    reduce_scatter x1, waiting for transfers between devices, per_device(): lax.psum_scatter(d_kv_all, 'batch', scatter_dimension=0, tiled=True)  83.5 us
    ppermute x4, waiting for transfers between devices, meet_target_up(): tile_out = lax.ppermute(tile_out, 'head', sheets)  71.5 us
    all_gather x1, waiting for transfers between devices, per_device(): mixed_all = lax.all_gather(mixed, 'head', axis=1, tiled=True)  55.6 us
    all_gather x1, waiting for transfers between devices, per_device(): out_full = lax.all_gather(out_own, 'head', axis=0, tiled=True)  52.8 us
    dot_general x7, matrix products, matmul(): return jnp.dot(left, right, preferred_element_type=F32)  52.7 us
  transfers between devices with their start and end apart: 27, of which 24 were waited for; matrix products, arithmetic and copies ran while one was open for 14% of the time, Pallas kernels for 0%

profile of v1, /device:TPU:0, one launch (start us, length us, event | category | flops | bytes accessed | tf_op | source)
XLA Modules:
  0.0 1140.4 jit_solution(11310236427097215450)
XLA Ops:
  9.3 3.0 collective-permute-start
  12.3 3.5 collective-permute-done
  19.5 5.2 all_gather.34
  24.7 3.9 multiply_reduce_fusion.1
  28.6 13.7 %all-gather.10.cloned.1.call-done = bf16[2048,512]{1,0:T(8,128)(2,1)} async-done(((bf16[512,512]{1,0:T(8,128)(2,1)}), bf16[2048,512]{1,0:T(8,128)(2,1)}) %all-gather.10.cloned.1.call-update) | async-done | bytes 2097168 | tf_op jit(solution)/shard_map/all_gather | solution.py:95
  42.3 7.8 fusion.167
  51.1 7.6 all_gather.38
  59.9 5.2 all-gather
  73.6 3.3 all-gather.12.cloned.1.call-done
  76.9 8.3 conditional.16
  76.9 3.0 copy.141
  82.2 2.9 select_reduce_fusion
  86.1 6.3 conditional.20
  86.1 3.1 copy.149
  89.2 3.2 fusion.10
  99.7 52.8 %all-gather.16.cloned.1.call-done = bf16[1024,2048]{1,0:T(8,128)(2,1)} async-done(((bf16[128,2048]{1,0:T(8,128)(2,1)}), bf16[1024,2048]{1,0:T(8,128)(2,1)}) %all-gather.16.cloned.1.call-update) | async-done | bytes 4194320 | tf_op jit(solution)/shard_map/all_gather | solution.py:100
  152.5 55.6 %all-gather.14.cloned.1.call-done = bf16[1280,1024]{0,1:T(8,128)(2,1)} async-done(((bf16[1280,128]{0,1:T(8,128)(2,1)}), bf16[1280,1024]{0,1:T(8,128)(2,1)}) %all-gather.14.cloned.1.call-update) | async-done | bytes 2621456 | tf_op jit(solution)/shard_map/all_gather | solution.py:166
  208.0 10.4 multiply_reduce_fusion
  218.5 4.0 copy-done.3
  222.5 3.3 multiply_convert_fusion
  225.7 10.8 all-gather.18.cloned.1.call-done
  236.6 9.6 fusion.168
  246.2 20.4 %all-gather.20.cloned.1.call-done = bf16[2048,768]{1,0:T(8,128)(2,1)} async-done(((bf16[512,768]{1,0:T(8,128)(2,1)}), bf16[2048,768]{1,0:T(8,128)(2,1)}) %all-gather.20.cloned.1.call-update) | async-done | bytes 3145744 | tf_op jit(solution)/shard_map/all_gather | solution.py:102
  266.5 9.6 fusion.169
  276.1 20.5 %all-gather.22.cloned.1.call-done = bf16[768,2048]{1,0:T(8,128)(2,1)} async-done(((bf16[768,512]{1,0:T(8,128)(2,1)}), bf16[768,2048]{1,0:T(8,128)(2,1)}) %all-gather.22.cloned.1.call-update) | async-done | bytes 3145744 | tf_op jit(solution)/shard_map/all_gather | solution.py:103
  296.7 13.6 %multiply_convert_fusion.2 = (bf16[1280,768]{1,0:T(8,128)(2,1)}, bf16[1280,768]{1,0:T(8,128)(2,1)S(1)}, bf16[1280,768]{1,0:T(8,128)(2,1)}) fusion(f32[1280,768]{1,0:T(8,128)} %fusion.168, f32[1280,768]{1,0:T(8,128)} %fusion.169, bf16[1280,2048]{1,0:T(8,128)(2,1)} %param.57, bf16[768,2048]{1,0:T(8,128)(2,1)} %all-gather.22.cloned.1.call-done), kind=kOutput, calls=%fused_computation.193 | convolution fusion | flops 4041277440 | bytes 22151168 | tf_op jit(solution)/shard_map/dot_general | solution.py:45
  310.3 4.3 fusion.170
  314.6 7.7 add_convert_fusion
  322.5 102.7 %reduce-scatter.12.cloned.1.call-done = bf16[160,2048]{1,0:T(8,128)(2,1)} async-done(((bf16[1280,2048]{1,0:T(8,128)(2,1)}), bf16[160,2048]{1,0:T(8,128)(2,1)}) %reduce-scatter.12.cloned.1.call-update) | async-done | bytes 655376 | tf_op jit(solution)/shard_map/reduce_scatter | solution.py:183
  433.3 4.5 all-to-all-start
  437.8 10.4 all-to-all-done
  453.8 8.0 conditional.24
  456.3 3.4 fusion.45
  462.2 13.4 %conditional.28 = (f32[1280,128]{1,0:T(8,128)}, bf16[1280,256]{0,1:T(8,128)(2,1)}) conditional(s32[]{:T(128)} %bitcast.4, () %tuple.134, (s32[1280]{0:T(1024)S(1)}, s32[5120]{0:T(1024)S(1)}, s32[1280]{0:T(1024)S(1)}, bf16[5120,256]{0,1:T(8,128)(2,1)S(1)}, bf16[1280,128]{0,1:T(8,128)(2,1)S(1)}, /*index=5*/f32[1280]{0:T(1024)S(1)}, ...), branch_computations={%region_41.42_spmd, %region_42.43_spmd} | conditional | flops 2116812800 | bytes 39685136 | solution.py:229
  464.8 3.5 fusion.72
  472.8 2.8 fusion.81
  477.6 7.3 conditional.31
  484.9 3.0 pad_maximum_fusion.5
  487.9 4.5 convolution_convert_fusion.6
  492.5 83.5 %reduce-scatter.14.cloned.1.call-done = bf16[1280,256]{0,1:T(8,128)(2,1)} async-done(((bf16[5120,256]{0,1:T(8,128)(2,1)}), bf16[1280,256]{0,1:T(8,128)(2,1)}) %reduce-scatter.14.cloned.1.call-update) | async-done | bytes 655376 | tf_op jit(solution)/shard_map/reduce_scatter | solution.py:232
  584.5 13.0 %collective-permute-done.8 = bf16[1280,256]{0,1:T(8,128)(2,1)S(1)} collective-permute-done((bf16[1280,256]{0,1:T(8,128)(2,1)}, bf16[1280,256]{0,1:T(8,128)(2,1)S(1)}, u32[]{:S(2)}, u32[]{:S(2)}) %collective-permute-start.8) | collective-permute-done | bytes 655392 | tf_op jit(solution)/shard_map/ppermute | solution.py:33
  597.7 6.8 convolution_convert_fusion.4
  604.9 9.2 convolution_convert_fusion.5
  614.2 9.1 convolution_convert_fusion.7
  623.5 7.7 convolution_convert_fusion.8
  631.2 7.2 convolution_convert_fusion.9
  638.4 3.8 pad_maximum_fusion.4
  642.3 26.8 %reduce-scatter.20.cloned.1.call-done = bf16[128,2048]{1,0:T(8,128)(2,1)} async-done(((bf16[1024,2048]{1,0:T(8,128)(2,1)}), bf16[128,2048]{1,0:T(8,128)(2,1)}) %reduce-scatter.20.cloned.1.call-update) | async-done | bytes 524304 | tf_op jit(solution)/shard_map/reduce_scatter | solution.py:200
  669.2 7.0 convolution_convert_fusion.10
  676.6 7.8 convert_element_type.190
  684.4 90.7 %reduce-scatter.16.cloned.1.call-done = bf16[160,2048]{1,0:T(8,128)(2,1)} async-done(((bf16[1280,2048]{1,0:T(8,128)(2,1)}), bf16[160,2048]{1,0:T(8,128)(2,1)}) %reduce-scatter.16.cloned.1.call-update) | async-done | bytes 655376 | tf_op jit(solution)/shard_map/reduce_scatter | solution.py:256
  777.0 2.8 fusion.141
  779.8 101.6 %reduce-scatter.10.cloned.1.call-done = bf16[160,2048]{1,0:T(8,128)(2,1)} async-done(((bf16[1280,2048]{1,0:T(8,128)(2,1)}), bf16[160,2048]{1,0:T(8,128)(2,1)}) %reduce-scatter.10.cloned.1.call-update) | async-done | bytes 655376 | tf_op jit(solution)/shard_map/reduce_scatter | solution.py:185
  881.4 3.0 broadcast_in_dim.124
  888.2 3.2 collective-permute-start.2
  891.5 24.7 %collective-permute-done.1 = bf16[160,2048]{1,0:T(8,128)(2,1)S(1)} collective-permute-done((bf16[160,2048]{1,0:T(8,128)(2,1)S(1)}, bf16[160,2048]{1,0:T(8,128)(2,1)S(1)}, u32[]{:S(2)}, u32[]{:S(2)}) %collective-permute-start.1) | collective-permute-done | bytes 655392 | tf_op jit(solution)/shard_map/ppermute | solution.py:22
  925.0 20.7 %collective-permute-done.3 = bf16[160,2048]{1,0:T(8,128)(2,1)S(1)} collective-permute-done((bf16[160,2048]{1,0:T(8,128)(2,1)S(1)}, bf16[160,2048]{1,0:T(8,128)(2,1)S(1)}, u32[]{:S(2)}, u32[]{:S(2)}) %collective-permute-start.3) | collective-permute-done | bytes 655392 | tf_op jit(solution)/shard_map/ppermute | solution.py:22
  953.2 21.4 %collective-permute-done.5 = bf16[160,2048]{1,0:T(8,128)(2,1)} collective-permute-done((bf16[160,2048]{1,0:T(8,128)(2,1)S(1)}, bf16[160,2048]{1,0:T(8,128)(2,1)}, u32[]{:S(2)}, u32[]{:S(2)}) %collective-permute-start.5) | collective-permute-done | bytes 655392 | tf_op jit(solution)/shard_map/ppermute | solution.py:22
  987.7 4.7 collective-permute-done.7
  994.4 12.3 %reduce-scatter.22.cloned.1.call-done = bf16[128,512]{1,0:T(8,128)(2,1)} async-done(((bf16[128,2048]{1,0:T(8,128)(2,1)}), bf16[128,512]{1,0:T(8,128)(2,1)}) %reduce-scatter.22.cloned.1.call-update) | async-done | bytes 131088 | tf_op jit(solution)/shard_map/reduce_scatter | solution.py:279
  1008.3 29.7 %reduce-scatter.18.cloned.1.call-done = bf16[512,384]{1,0:T(8,128)(2,1)} async-done(((bf16[2048,384]{1,0:T(8,128)(2,1)}), bf16[512,384]{1,0:T(8,128)(2,1)}) %reduce-scatter.18.cloned.1.call-update) | async-done | bytes 393232 | tf_op jit(solution)/shard_map/reduce_scatter | solution.py:278
  1042.4 40.9 %psum.7 = f32[2,2048]{1,0:T(2,128)S(1)} all-reduce(f32[2,2048]{1,0:T(2,128)S(1)} %pad_maximum_fusion.11), channel_id=1, replica_groups=mesh['batch'=4,'head'=8] {'batch','head'}, use_global_device_ids=true, to_apply=%region_54.55 | all-reduce | flops 4096 | bytes 32768 | tf_op jit(solution)/shard_map/psum | solution.py:280
  1084.0 43.9 %all-gather.24.cloned.1.call-done = bf16[1280,2048]{1,0:T(8,128)(2,1)} async-done(((bf16[160,2048]{1,0:T(8,128)(2,1)}), bf16[1280,2048]{1,0:T(8,128)(2,1)}) %all-gather.24.cloned.1.call-update) | async-done | bytes 5242896 | tf_op jit(solution)/shard_map/all_gather | solution.py:266
  1127.9 5.7 copy.277
  (175 shorter events, 104.6 us)
Async XLA Ops:
  7.2 35.1 %all-gather.10.cloned.1.call-start = ((), (), s32[]{:S(2)}) async-start(), calls=%async_computation.10 | async-start | bytes 2621440 | tf_op jit(solution)/shard_map/all_gather | solution.py:95
  9.3 6.5 collective-permute-start
  18.1 58.8 %all-gather.12.cloned.1.call-start = ((), (), s32[]{:S(2)}) async-start(), calls=%async_computation.11 | async-start | bytes 3276800 | tf_op jit(solution)/shard_map/all_gather | solution.py:112
  28.6 21.6 %copy-start.15 = (f32[1280]{0:T(1024)}, f32[1280]{0:T(1024)S(1)}, u32[]{:S(2)}) copy-start(f32[1280]{0:T(1024)S(1)} %add_rsqrt_fusion.1) | copy-start | bytes 15364
  28.6 21.5 %copy-start.12 = (f32[1,2048]{1,0:T(1,128)}, f32[1,2048]{1,0:T(1,128)S(1)}, u32[]{:S(2)}) copy-start(f32[1,2048]{1,0:T(1,128)S(1)} %get-tuple-element.895) | copy-start | bytes 24580
  42.3 8.8 copy-start.11
  42.3 16.5 %copy-start.10 = (s32[1280]{0:T(1024)S(1)}, s32[1280]{0:T(1024)}, u32[]{:S(2)}) copy-start(s32[1280]{0:T(1024)} %param.46) | copy-start | bytes 15364
  51.0 101.4 %all-gather.16.cloned.1.call-start = ((), (), s32[]{:S(2)}) async-start(), calls=%async_computation.13 | async-start | bytes 4718592 | tf_op jit(solution)/shard_map/all_gather | solution.py:100
  58.8 149.3 %all-gather.14.cloned.1.call-start = ((), (), s32[]{:S(2)}) async-start(), calls=%async_computation.12 | async-start | bytes 2949120 | tf_op jit(solution)/shard_map/all_gather | solution.py:166
  95.4 123.0 %copy-start.4 = (f32[1280,128]{0,1:T(8,128)}, f32[1280,128]{0,1:T(8,128)S(1)}, u32[]{:S(2)}) copy-start(f32[1280,128]{0,1:T(8,128)S(1)} %get-tuple-element.854) | copy-start | bytes 1966084
  97.7 138.8 %all-gather.18.cloned.1.call-start = ((), (), s32[]{:S(2)}) async-start(), calls=%async_computation.14 | async-start | bytes 3932160 | tf_op jit(solution)/shard_map/all_gather | solution.py:101
  98.3 168.2 %all-gather.20.cloned.1.call-start = ((), (), s32[]{:S(2)}) async-start(), calls=%async_computation.15 | async-start | bytes 3932160 | tf_op jit(solution)/shard_map/all_gather | solution.py:102
  98.9 197.8 %all-gather.22.cloned.1.call-start = ((), (), s32[]{:S(2)}) async-start(), calls=%async_computation.16 | async-start | bytes 3932160 | tf_op jit(solution)/shard_map/all_gather | solution.py:103
  99.6 325.5 %reduce-scatter.12.cloned.1.call-start = ((), (), s32[]{:S(2)}) async-start(), calls=%async_computation.18 | async-start | bytes 5898240 | tf_op jit(solution)/shard_map/reduce_scatter | solution.py:183
  218.4 4.0 copy-start.3
  296.7 13.6 %copy-start.17 = (bf16[2048,768]{1,0:T(8,128)(2,1)S(1)}, bf16[2048,768]{1,0:T(8,128)(2,1)}, u32[]{:S(2)}) copy-start(bf16[2048,768]{1,0:T(8,128)(2,1)} %all-gather.18.cloned.1.call-done) | copy-start | bytes 9437188
  310.3 4.3 copy-start.19
  310.3 4.3 copy-start.18
  425.2 5.8 copy-start.5
  429.9 1.1 copy-start.1
  432.5 21.3 %copy-start = (bf16[5120,256]{0,1:T(8,128)(2,1)S(1)}, bf16[5120,256]{0,1:T(8,128)(2,1)}, u32[]{:S(2)}) copy-start(bf16[5120,256]{0,1:T(8,128)(2,1)} %all-gather.12.cloned.1.call-done) | copy-start | bytes 7864324
  433.3 15.0 %all-to-all-start = ((bf16[160,8,128]{2,0,1:T(8,128)(2,1)}), bf16[160,8,128]{2,0,1:T(8,128)(2,1)S(1)}, u32[]{:S(2)}, u32[]{:S(2)}) async-start(bf16[160,8,128]{2,0,1:T(8,128)(2,1)} %bitcast.84), calls=%async_computation.2 | async-start | bytes 655360 | tf_op jit(solution)/shard_map/all_to_all | solution.py:196
  437.8 138.3 %reduce-scatter.14.cloned.1.call-start = ((), (), s32[]{:S(2)}) async-start(), calls=%async_computation.19 | async-start | bytes 3276800 | tf_op jit(solution)/shard_map/reduce_scatter | solution.py:232
  484.9 3.1 copy-start.2
  487.9 181.3 %reduce-scatter.20.cloned.1.call-start = ((), (), s32[]{:S(2)}) async-start(), calls=%async_computation.23 | async-start | bytes 4718592 | tf_op jit(solution)/shard_map/reduce_scatter | solution.py:200
  492.5 105.2 %copy-start.8 = (bf16[1280,128]{0,1:T(8,128)(2,1)S(1)}, bf16[1280,128]{0,1:T(8,128)(2,1)}, u32[]{:S(2)}) copy-start(bf16[1280,128]{0,1:T(8,128)(2,1)} %get-tuple-element.873) | copy-start | bytes 983044
  492.5 282.6 %reduce-scatter.16.cloned.1.call-start = ((), (), s32[]{:S(2)}) async-start(), calls=%async_computation.20 | async-start | bytes 5898240 | tf_op jit(solution)/shard_map/reduce_scatter | solution.py:256
  576.1 21.4 %copy-start.7 = (bf16[1280,256]{0,1:T(8,128)(2,1)S(1)}, bf16[1280,256]{0,1:T(8,128)(2,1)}, u32[]{:S(2)}) copy-start(bf16[1280,256]{0,1:T(8,128)(2,1)} %reduce-scatter.14.cloned.1.call-done) | copy-start | bytes 1966084
  576.1 21.4 %collective-permute-start.8 = (bf16[1280,256]{0,1:T(8,128)(2,1)}, bf16[1280,256]{0,1:T(8,128)(2,1)S(1)}, u32[]{:S(2)}, u32[]{:S(2)}) collective-permute-start(bf16[1280,256]{0,1:T(8,128)(2,1)} %reduce-scatter.14.cloned.1.call-done), channel_id=1, source_target_pairs={{0,1},{1,0},{2,3},{3,2},{4,5},{5,4},{6,7},{7,6},{8,9},{9,8},{10,11... | collective-permute-start | bytes 1966088 | tf_op jit(solution)/shard_map/ppermute | solution.py:33
  604.5 276.9 %reduce-scatter.10.cloned.1.call-start = ((), (), s32[]{:S(2)}) async-start(), calls=%async_computation.17 | async-start | bytes 5898240 | tf_op jit(solution)/shard_map/reduce_scatter | solution.py:185
  614.2 307.5 %reduce-scatter.26.cloned.1.call-start = ((), (), s32[]{:S(2)}) async-start(), calls=%async_computation.26 | async-start | bytes 3932160 | tf_op jit(solution)/shard_map/reduce_scatter | solution.py:276
  623.3 359.3 %reduce-scatter.24.cloned.1.call-start = ((), (), s32[]{:S(2)}) async-start(), calls=%async_computation.25 | async-start | bytes 7864320 | tf_op jit(solution)/shard_map/reduce_scatter | solution.py:274
  623.5 7.7 copy-start.20
  642.2 27.0 %copy-start.9 = (bf16[1280,128]{0,1:T(8,128)(2,1)S(1)}, bf16[1280,128]{0,1:T(8,128)(2,1)}, u32[]{:S(2)}) copy-start(bf16[1280,128]{0,1:T(8,128)(2,1)} %copy.184) | copy-start | bytes 983044
  642.2 27.0 %copy-start.13 = (f32[1,2048]{1,0:T(1,128)S(1)}, f32[1,2048]{1,0:T(1,128)}, u32[]{:S(2)}) copy-start(f32[1,2048]{1,0:T(1,128)} %copy-done.12) | copy-start | bytes 24580
  642.2 27.0 %copy-start.16 = (f32[1280]{0:T(1024)S(1)}, f32[1280]{0:T(1024)}, u32[]{:S(2)}) copy-start(f32[1280]{0:T(1024)} %copy-done.15) | copy-start | bytes 15364
  642.3 364.4 %reduce-scatter.22.cloned.1.call-start = ((), (), s32[]{:S(2)}) async-start(), calls=%async_computation.24 | async-start | bytes 655360 | tf_op jit(solution)/shard_map/reduce_scatter | solution.py:279
  669.2 368.8 %reduce-scatter.18.cloned.1.call-start = ((), (), s32[]{:S(2)}) async-start(), calls=%async_computation.22 | async-start | bytes 1966080 | tf_op jit(solution)/shard_map/reduce_scatter | solution.py:278
  676.2 451.7 %all-gather.24.cloned.1.call-start = ((), (), s32[]{:S(2)}) async-start(), calls=%async_computation.21 | async-start | bytes 5898240 | tf_op jit(solution)/shard_map/all_gather | solution.py:266
  881.4 3.0 copy-start.6
  886.7 29.4 %collective-permute-start.1 = (bf16[160,2048]{1,0:T(8,128)(2,1)S(1)}, bf16[160,2048]{1,0:T(8,128)(2,1)S(1)}, u32[]{:S(2)}, u32[]{:S(2)}) collective-permute-start(bf16[160,2048]{1,0:T(8,128)(2,1)S(1)} %get-tuple-element.860), channel_id=1, source_target_pairs={{0,1},{1,2},{2,3},{3,4},{4,5},{5,6},{6,7},{7,0},{8,9},{9,10},{10,1... | collective-permute-start | bytes 1966088 | tf_op jit(solution)/shard_map/ppermute | solution.py:22
  888.2 30.4 %collective-permute-start.2 = (bf16[160,2048]{1,0:T(8,128)(2,1)S(1)}, bf16[160,2048]{1,0:T(8,128)(2,1)S(1)}, u32[]{:S(2)}, u32[]{:S(2)}) collective-permute-start(bf16[160,2048]{1,0:T(8,128)(2,1)S(1)} %get-tuple-element.860), channel_id=1, source_target_pairs={{0,7},{1,0},{2,1},{3,2},{4,3},{5,4},{6,5},{7,6},{8,15},{9,8},{10,9... | collective-permute-start | bytes 1966088 | tf_op jit(solution)/shard_map/ppermute | solution.py:25
  916.1 29.6 %collective-permute-start.3 = (bf16[160,2048]{1,0:T(8,128)(2,1)S(1)}, bf16[160,2048]{1,0:T(8,128)(2,1)S(1)}, u32[]{:S(2)}, u32[]{:S(2)}) collective-permute-start(bf16[160,2048]{1,0:T(8,128)(2,1)S(1)} %collective-permute-done.1), channel_id=1, source_target_pairs={{0,1},{1,2},{2,3},{3,4},{4,5},{5,6},{6,7},{7,0},{8,9},{9,10},{10,1... | collective-permute-start | bytes 1966088 | tf_op jit(solution)/shard_map/ppermute | solution.py:22
  918.6 30.5 %collective-permute-start.4 = (bf16[160,2048]{1,0:T(8,128)(2,1)S(1)}, bf16[160,2048]{1,0:T(8,128)(2,1)S(1)}, u32[]{:S(2)}, u32[]{:S(2)}) collective-permute-start(bf16[160,2048]{1,0:T(8,128)(2,1)S(1)} %collective-permute-done.2), channel_id=1, source_target_pairs={{0,7},{1,0},{2,1},{3,2},{4,3},{5,4},{6,5},{7,6},{8,15},{9,8},{10,9... | collective-permute-start | bytes 1966088 | tf_op jit(solution)/shard_map/ppermute | solution.py:25
  945.8 28.8 %collective-permute-start.5 = (bf16[160,2048]{1,0:T(8,128)(2,1)S(1)}, bf16[160,2048]{1,0:T(8,128)(2,1)}, u32[]{:S(2)}, u32[]{:S(2)}) collective-permute-start(bf16[160,2048]{1,0:T(8,128)(2,1)S(1)} %collective-permute-done.3), channel_id=1, source_target_pairs={{0,1},{1,2},{2,3},{3,4},{4,5},{5,6},{6,7},{7,0},{8,9},{9,10},{10,1... | collective-permute-start | bytes 1966088 | tf_op jit(solution)/shard_map/ppermute | solution.py:22
  949.1 30.0 %collective-permute-start.6 = (bf16[160,2048]{1,0:T(8,128)(2,1)S(1)}, bf16[160,2048]{1,0:T(8,128)(2,1)S(1)}, u32[]{:S(2)}, u32[]{:S(2)}) collective-permute-start(bf16[160,2048]{1,0:T(8,128)(2,1)S(1)} %collective-permute-done.4), channel_id=1, source_target_pairs={{0,7},{1,0},{2,1},{3,2},{4,3},{5,4},{6,5},{7,6},{8,15},{9,8},{10,9... | collective-permute-start | bytes 1966088 | tf_op jit(solution)/shard_map/ppermute | solution.py:25
  974.6 17.8 %collective-permute-start.7 = (bf16[160,2048]{1,0:T(8,128)(2,1)}, bf16[160,2048]{1,0:T(8,128)(2,1)}, u32[]{:S(2)}, u32[]{:S(2)}) collective-permute-start(bf16[160,2048]{1,0:T(8,128)(2,1)} %collective-permute-done.5), channel_id=1, source_target_pairs={{0,1},{1,2},{2,3},{3,4},{4,5},{5,6},{6,7},{7,0},{8,9},{9,10},{10,1... | collective-permute-start | bytes 1966088 | tf_op jit(solution)/shard_map/ppermute | solution.py:22
  986.0 56.4 %copy-start.14 = (f32[2048]{0:T(1024)S(1)}, f32[2048]{0:T(1024)}, u32[]{:S(2)}) copy-start(f32[2048]{0:T(1024)} %get-tuple-element.857) | copy-start | bytes 24580
Sparse Core Ops, SparseCore 0:
  18.2 24.0 all-gather.9
  51.1 25.6 all-gather.11
  79.0 73.4 all-gather.15
  155.1 52.9 all-gather.13
  209.4 27.0 all-gather.17
  238.0 28.5 all-gather.19
  268.1 28.5 all-gather.21
  322.5 102.5 reduce-scatter.11
  488.0 88.0 reduce-scatter.13
  580.0 89.1 reduce-scatter.19
  672.7 102.2 reduce-scatter.15
  779.1 102.2 reduce-scatter.9
  883.9 37.6 reduce-scatter.25
  924.2 58.3 reduce-scatter.23
  984.9 21.6 reduce-scatter.21
  1009.8 28.1 reduce-scatter.17
  1040.0 87.8 all-gather.23
